TPU v7x, 1024 devices: a whole 4x8x16 slice. The times are simulated.
1024 devices in a mesh: rows: 128 (over x, y, z_lo), aux: 8 (over z_hi, core).
Axes of the slice: x: 4, y: 8, z: 16 (z_hi: 4, z_lo: 4; z = z_hi * 4 + z_lo), core: 2. Of those that a mesh axis runs over, the one named last changes fastest.
Arguments:
- pair_green_block: bfloat16 [65536, 2048], P('rows', 'aux'), may hold values from -6 to 6
- cholesky_factors: bfloat16 [65536, 512], P('rows', 'aux'), may hold values from -0.09375 to 0.09375
- green_one: float32 [256, 256], replicated, may hold values from -0.375 to 0.375
- screening: float32 [512], replicated, may hold values from 0.25 to 4
Outputs:
- section_slope: float32 [65536, 2048], P('rows', 'aux')
- collision: float32 [65536], P(('rows', 'aux'))
All inputs are finite; a program needn't handle non-finite values.
Results may differ from a plain program's by a relative error of at most 0.0029.
Values may be sent and summed in bfloat16 or wider, within the bound.
A program may use at most 32 MiB of HBM per device.

v0:
```python
import jax
import jax.numpy as jnp
from jax import lax
from jax.sharding import PartitionSpec as P

NORB = 256


def dress_aux(projected, green_one, screening):
    vec_count = projected.shape[0]
    block_pair_columns = projected.shape[1]
    shaped = projected.reshape(vec_count, block_pair_columns // NORB, NORB)
    dressed = jnp.einsum("qkm,ml->qkl", shaped, green_one, precision=lax.Precision.HIGHEST)
    return (
        (dressed * screening[:, None, None])
        .reshape(vec_count, block_pair_columns)
        .astype(jnp.bfloat16)
    )


def local(pair_green_block, cholesky_factors, green_one, screening):
    highest = lax.Precision.HIGHEST
    block_pair_columns = pair_green_block.shape[1]
    orb_count = block_pair_columns // NORB
    chol_basis = lax.all_gather(cholesky_factors, "aux", axis=1, tiled=True)
    partial_projection = lax.dot_general(
        chol_basis, pair_green_block, (((0,), (0,)), ((), ())), preferred_element_type=jnp.float32
    )
    projected = lax.psum(partial_projection, "rows")
    dressed = dress_aux(projected, green_one, screening)
    section_slope = jnp.dot(chol_basis, dressed, preferred_element_type=jnp.float32)
    first_orb = lax.axis_index("aux") * orb_count
    green_function_columns = lax.dynamic_slice_in_dim(green_one, first_orb, orb_count, 1)
    trace_weights = green_function_columns.T.reshape(block_pair_columns)
    partial_collision = jnp.dot(
        section_slope, trace_weights, precision=highest, preferred_element_type=jnp.float32
    )
    collision = lax.psum_scatter(partial_collision, "aux", scatter_dimension=0, tiled=True)
    return (section_slope, collision)


def solution(mesh):
    placed = (P("rows", "aux"), P("rows", "aux"), P(), P())
    return jax.shard_map(
        local,
        mesh=mesh,
        in_specs=placed,
        out_specs=(P("rows", "aux"), P(("rows", "aux"))),
        check_vma=False,
    )
```

profile of v0, /device:TPU:1, one launch (start us, length us, event | category | flops | bytes accessed | tf_op | source)
XLA Modules:
  0.0 1394.2 jit_solution(781443843832033934)
XLA Ops:
  7.2 0.0 copy-start
  7.2 0.0 copy-start.1
  7.2 0.0 all-reduce.3.cloned.1.call-start
  7.2 34.1 %all_gather.3 = bf16[512,512]{0,1:T(8,128)(2,1)S(1)} all-gather(bf16[512,64]{0,1:T(8,128)(2,1)} %param.5), channel_id=1, replica_groups=mesh['rows'=128,'aux'=8] {'aux'}, dimensions={1}, use_global_device_ids=true | all-gather | bytes 589824 | tf_op jit(solution)/shard_map/all_gather | solution.py:25
  41.3 0.0 copy-done.1
  41.3 1.1 fusion.1
  42.4 0.0 all-reduce.3.cloned.1.call-update
  42.5 1.3 dynamic-slice
  44.4 0.0 copy-done
  44.4 0.0 copy-start.2
  44.4 0.2 dynamic-slice_reduce_fusion
  44.6 1265.2 %all-reduce.3.cloned.1.call-done = f32[512,256]{1,0:T(8,128)} async-done(((f32[512,256]{1,0:T(8,128)}), f32[512,256]{1,0:T(8,128)}) %all-reduce.3.cloned.1.call-update) | async-done | bytes 524304 | tf_op jit(solution)/shard_map/psum | solution.py:29
  1309.8 0.0 copy-done.2
  1309.8 1.6 fusion
  1311.4 0.3 convolution_bitcast_fusion
  1311.7 1.0 copy.8
  1312.7 0.4 fusion.2
  1313.1 73.6 %all-reduce = f32[512]{0:T(512)S(1)} all-reduce(f32[512]{0:T(512)S(1)} %bitcast.13), channel_id=2, replica_groups=mesh['rows'=128,'aux'=8] {'aux'}, use_global_device_ids=true, to_apply=%region_1.0.clone | all-reduce | flops 512 | bytes 4096
  1386.7 0.6 dynamic-slice.1
Async XLA Ops:
  7.2 37.2 %copy-start = (f32[256,256]{1,0:T(8,128)S(1)}, f32[256,256]{1,0:T(8,128)}, u32[]{:S(2)}) copy-start(f32[256,256]{1,0:T(8,128)} %param.6) | copy-start | bytes 786436
  7.2 34.2 %copy-start.1 = (bf16[512,256]{1,0:T(8,128)(2,1)S(1)}, bf16[512,256]{1,0:T(8,128)(2,1)}, u32[]{:S(2)}) copy-start(bf16[512,256]{1,0:T(8,128)(2,1)} %param.4) | copy-start | bytes 786436
  7.2 1302.6 %all-reduce.3.cloned.1.call-start = ((), (), s32[]{:S(2)}) async-start(), calls=%async_computation | async-start | bytes 1048576 | tf_op jit(solution)/shard_map/psum | solution.py:29
  44.4 1265.4 %copy-start.2 = (f32[512]{0:T(512)S(1)}, f32[512]{0:T(512)}, u32[]{:S(2)}) copy-start(f32[512]{0:T(512)} %param.7) | copy-start | bytes 6148
Sparse Core Ops, SparseCore 0:
  42.6 1267.1 all-reduce.2
where the time goes:
time: 1390 us
  waiting for transfers between devices  1270 us (91%)
  blocking collectives  108 us (8%)
  between operations  14.7 us (1%)
    psum x1, waiting for transfers between devices, local(): projected = lax.psum(partial_projection, 'rows')  1270 us
    unnamed x1, blocking collectives  73.6 us
    all_gather x1, blocking collectives, local(): chol_basis = lax.all_gather(cholesky_factors, 'aux', axis=1, tiled=True)  34.1 us
  transfers between devices with their start and end apart: 1, of which 1 were waited for; matrix products, arithmetic and copies ran while one was open for 0% of the time, Pallas kernels for 0%

commit v1 on v0

v1 whole, which is shorter than its diff:
```python
import jax
import jax.numpy as jnp
from jax import lax
from jax.experimental import pallas as pl
from jax.experimental.pallas import tpu as pltpu
from jax.sharding import PartitionSpec as P

NX, NY, NZ, NH = 4, 8, 4, 4
F32, BF16 = jnp.float32, jnp.bfloat16
HIGHEST = lax.Precision.HIGHEST
NT = (((1,), (1,)), ((), ()))
NN = (((1,), (0,)), ((), ()))


def dot(a, b, dims=NN, precision=None):
    return lax.dot_general(a, b, dims, precision=precision, preferred_element_type=F32)


def iota(shape, axis):
    return lax.broadcasted_iota(jnp.int32, shape, axis)


def kernel(
    green_block, own_chol, green_one, screening, slope, collision,
    chol_t, part, part_in, ysum, y_in, z_all, dressed, chol_p, vec, vx, vy, vz, vh, vc,
    pc_send, pc_recv, z_send, z_recv, f_send, f_recv, x_send, x_recv, y_send, y_recv,
    l_send, l_recv, gy_send, gy_recv, gx_send, gx_recv,
    vx_send, vx_recv, vy_send, vy_recv, vz_send, vz_recv, vh_send, vh_recv, vc_send, vc_recv,
):
    row, aux = lax.axis_index("rows"), lax.axis_index("aux")
    mx, my, mz = row // (NY * NZ), (row // NZ) % NY, row % NZ
    mh, core = aux // 2, aux % 2

    def at_x(j):
        return {"rows": (((mx + j) % NX) * NY + my) * NZ + mz, "aux": aux}

    def at_y(j):
        return {"rows": (mx * NY + (my + j) % NY) * NZ + mz, "aux": aux}

    def at_z(j):
        return {"rows": (mx * NY + my) * NZ + (mz + j) % NZ, "aux": aux}

    def at_h(j):
        return {"rows": row, "aux": ((mh + j) % NH) * 2 + core}

    mate = {"rows": row, "aux": mh * 2 + 1 - core}
    sent = []

    def copy(src, dst, send, recv, to):
        made = pltpu.make_async_remote_copy(
            src_ref=src, dst_ref=dst, send_sem=send, recv_sem=recv,
            device_id=to, device_id_type=pl.DeviceIdType.MESH,
        )
        return made

    def send(*what):
        made = copy(*what)
        made.start()
        sent.append(made)

    chol_t[0, core] = own_chol[...]
    barrier = pltpu.get_barrier_semaphore()
    peers = [mate] + [at_x(j) for j in range(1, NX)] + [at_y(j) for j in range(1, NY)]
    peers += [at_z(j) for j in range(1, NZ)] + [at_h(j) for j in range(1, NH)]
    for peer in peers:
        pl.semaphore_signal(barrier, inc=1, device_id=peer, device_id_type=pl.DeviceIdType.MESH)
    pl.semaphore_wait(barrier, len(peers))

    half = 32
    for i in range(2):
        rows_i = pl.ds(i * half, half)
        for slot, step in ((1, 1), (2, -1)):
            send(own_chol.at[rows_i], chol_t.at[slot, core, rows_i], z_send.at[slot, i], z_recv.at[slot, i], at_h(step))
    send(own_chol, chol_t.at[0, core], pc_send.at[0, 0], pc_recv.at[0, 0], mate)

    def z_block(slot, i):
        rows_i = pl.ds(i * half, half)
        here = chol_t.at[slot, core, rows_i]
        return here, z_recv.at[slot, i]

    def await_z(slot, i):
        here, sem = z_block(slot, i)
        copy(here, here, z_send.at[slot, i], sem, mate).wait_recv()

    def to_mate(slot, i):
        here, _ = z_block(slot, i)
        send(here, here, pc_send.at[slot, i], pc_recv.at[slot, i], mate)

    def from_mate(slot, i):
        there = chol_t.at[slot, 1 - core, pl.ds(i * half, half)]
        copy(there, there, pc_send.at[slot, i], pc_recv.at[slot, i], mate).wait_recv()

    pick = (iota((8, 256), 1) == aux).astype(F32)
    column = dot(pick, green_one[...], NT, HIGHEST)
    trace_row = dot(column, green_one[...], NT, HIGHEST)

    slot_h = [mh, (mh + NH - 1) % NH, (mh + 1) % NH, (mh + 2) % NH]
    top = iota((8, 128), 0) < 4
    lane, sub = iota((8, 128), 1), iota((8, 128), 0)
    own_first = 4 * (mx * NY + my)
    scales = []
    for t in range(4):
        weights = jnp.broadcast_to(screening[pl.ds(slot_h[t], 1), :], (8, 128))
        scales.append(jnp.sum(jnp.where(lane == own_first + sub % 4, weights, 0.0), axis=1, keepdims=True))

    vec[...] = jnp.zeros((8, 128), F32)

    def project(t):
        block = dot(chol_t[t].reshape(128, 512), green_block[...])
        for j in range(16):
            left, right = block[8 * j : 8 * j + 8, :128], block[8 * j : 8 * j + 8, 128:]
            for e in range(2):
                g = 2 * j + e
                if e == 0:
                    tile = jnp.where(top, left, pltpu.roll(right, 4, 0))
                else:
                    tile = jnp.where(top, pltpu.roll(left, 4, 0), right)
                part[t, g // NY, g % NY] = tile
        for j in range(1, NX):
            send(part.at[t, (mx + j) % NX], part_in.at[t, j], x_send.at[t, j], x_recv.at[t, j], at_x(j))
        terms = dot(trace_row, block, NT, HIGHEST)
        vec[...] = jnp.where(sub == slot_h[t], terms, vec[...])

    def sum_x(t):
        total = part[t, mx]
        for j in range(1, NX):
            copy(part_in.at[t, j], part_in.at[t, j], x_send.at[t, j], x_recv.at[t, j], mate).wait_recv()
            total = total + part_in[t, j]
        ysum[t] = total
        for j in range(1, NY):
            send(ysum.at[t, (my + j) % NY], y_in.at[t, j], y_send.at[t, j], y_recv.at[t, j], at_y(j))

    def sum_y(t):
        total = ysum[t, my]
        for j in range(1, NY):
            copy(y_in.at[t, j], y_in.at[t, j], y_send.at[t, j], y_recv.at[t, j], mate).wait_recv()
            total = total + y_in[t, j]
        z_all[mz, t] = total
        for j in range(1, NZ):
            send(z_all.at[mz, t], z_all.at[mz, t], l_send.at[t, j], l_recv.at[t, j], at_z(j))

    def spread(value, store, sems, count, to):
        store[0] = value
        for j in range(1, count):
            send(store.at[0], store.at[j], sems[0].at[j], sems[1].at[j], to(j))

    def collect(store, sems, count):
        total = store[0]
        for j in range(1, count):
            copy(store.at[j], store.at[j], sems[0].at[j], sems[1].at[j], mate).wait_recv()
            total = total + store[j]
        return total

    from_mate_0 = chol_t.at[0, 1 - core]
    copy(from_mate_0, from_mate_0, pc_send.at[0, 0], pc_recv.at[0, 0], mate).wait_recv()
    project(0)

    far, near = 1 + core, 2 - core
    for i in range(2):
        await_z(far, i)
        here, _ = z_block(far, i)
        onward = {"rows": row, "aux": ((mh + 1 + 2 * core) % NH) * 2 + core}
        send(here, chol_t.at[3, core, pl.ds(i * half, half)], f_send.at[i], z_recv.at[3, i], onward)
        to_mate(far, i)
        await_z(near, i)
        to_mate(near, i)
    sum_x(0)
    for slot in (1, 2):
        for i in range(2):
            from_mate(slot, i)
        project(slot)
    for i in range(2):
        await_z(3, i)
        to_mate(3, i)
    for i in range(2):
        from_mate(3, i)
    project(3)
    sems_vx, sems_vy, sems_vz, sems_vh = (vx_send, vx_recv), (vy_send, vy_recv), (vz_send, vz_recv), (vh_send, vh_recv)
    spread(vec[...], vx, sems_vx, NX, at_x)
    sum_y(0)
    sum_x(1)
    sum_x(2)

    for b in range(4):
        new = iota((128, 512), 0) + 128 * b
        old = ((new >> 2) & 3) * 128 + (new >> 7) * 32 + ((new >> 4) & 7) * 4 + (new & 3)
        move = jnp.where(iota((128, 512), 1) == old, 1.0, 0.0).astype(BF16)
        moved = dot(move, chol_t[...].reshape(512, 512))
        chol_p[:, 128 * b : 128 * b + 128] = moved.T.astype(BF16)

    sum_x(3)
    spread(collect(vx, sems_vx, NX), vy, sems_vy, NY, at_y)
    sum_y(1)
    sum_y(2)
    sum_y(3)
    spread(collect(vy, sems_vy, NY), vz, sems_vz, NZ, at_z)

    for t in range(4):
        for j in range(1, NZ):
            there = z_all.at[(mz + NZ - j) % NZ, t]
            copy(there, there, l_send.at[t, j], l_recv.at[t, j], mate).wait_recv()
    total = (z_all[0] + z_all[1]) + (z_all[2] + z_all[3])
    flat = total.reshape(32, 128)
    upper = dot(flat, green_one[:128, :], NN, HIGHEST)
    lower = dot(flat, green_one[128:, :], NN, HIGHEST)
    done = []
    for t in range(4):
        both = upper[8 * t : 8 * t + 8] + pltpu.roll(lower[8 * t : 8 * t + 8], 4, 0)
        done.append(both * scales[t])
    top2 = iota((8, 256), 0) < 4
    first = jnp.where(top2, done[0], pltpu.roll(done[1], 4, 0))
    second = jnp.where(top2, done[2], pltpu.roll(done[3], 4, 0))
    dressed[mx, my] = jnp.concatenate([first, second], axis=0).astype(BF16)

    for j in range(1, NY):
        here = dressed.at[mx, my]
        send(here, here, gy_send.at[j], gy_recv.at[j], at_y(j))
    spread(collect(vz, sems_vz, NZ), vh, sems_vh, NH, at_h)
    for j in range(1, NY):
        there = dressed.at[mx, (my + NY - j) % NY]
        copy(there, there, gy_send.at[j], gy_recv.at[j], mate).wait_recv()
    for j in range(1, NX):
        here = dressed.at[mx]
        send(here, here, gx_send.at[j], gx_recv.at[j], at_x(j))
    for j in range(1, NX):
        there = dressed.at[(mx + NX - j) % NX]
        copy(there, there, gx_send.at[j], gx_recv.at[j], mate).wait_recv()
    vc[0] = collect(vh, sems_vh, NH)
    send(vc.at[0], vc.at[1], vc_send, vc_recv, mate)

    slope[...] = dot(chol_p[...], dressed[...].reshape(512, 256))

    copy(vc.at[1], vc.at[1], vc_send, vc_recv, mate).wait_recv()
    vec[...] = vc[0] + vc[1]
    traced = jnp.zeros((8, 512), F32)
    for t in range(4):
        weights = vec[pl.ds(slot_h[t], 1), :] * screening[pl.ds(slot_h[t], 1), :]
        weights = jnp.broadcast_to(weights, (8, 128))
        traced = traced + dot(weights, chol_t[t].reshape(128, 512).astype(F32), NN, HIGHEST)
    for a in range(2 * NH):
        @pl.when(aux == a)
        def _():
            collision[...] = traced[0:1, 64 * a : 64 * a + 64]

    for made in sent:
        made.wait_send()


def local(pair_green_block, cholesky_factors, green_one, screening):
    vmem, dma = pltpu.VMEM, pltpu.SemaphoreType.DMA
    slope, collision = pl.pallas_call(
        kernel,
        out_shape=(jax.ShapeDtypeStruct((512, 256), F32), jax.ShapeDtypeStruct((1, 64), F32)),
        in_specs=[pl.BlockSpec(memory_space=vmem)] * 4,
        out_specs=(pl.BlockSpec(memory_space=vmem), pl.BlockSpec(memory_space=vmem)),
        scratch_shapes=[
            vmem((4, 2, 64, 512), BF16),
            vmem((4, NX, NY, 8, 128), F32),
            vmem((4, NX, NY, 8, 128), F32),
            vmem((4, NY, 8, 128), F32),
            vmem((4, NY, 8, 128), F32),
            vmem((NZ, 4, 8, 128), F32),
            vmem((NX, NY, 16, 256), BF16),
            vmem((512, 512), BF16),
            vmem((8, 128), F32),
            vmem((NX, 8, 128), F32),
            vmem((NY, 8, 128), F32),
            vmem((NZ, 8, 128), F32),
            vmem((NH, 8, 128), F32),
            vmem((2, 8, 128), F32),
            dma((4, 2)), dma((4, 2)), dma((4, 2)), dma((4, 2)), dma((2,)), dma((2,)),
            dma((4, NX)), dma((4, NX)), dma((4, NY)), dma((4, NY)),
            dma((4, NZ)), dma((4, NZ)), dma((NY,)), dma((NY,)), dma((NX,)), dma((NX,)),
            dma((NX,)), dma((NX,)), dma((NY,)), dma((NY,)), dma((NZ,)), dma((NZ,)),
            dma((NH,)), dma((NH,)), dma, dma,
        ],
        compiler_params=pltpu.CompilerParams(collective_id=0, has_side_effects=True),
    )(pair_green_block, cholesky_factors.T, green_one, screening.reshape(4, 128))
    return slope, collision.reshape(64)


def solution(mesh):
    placed = (P("rows", "aux"), P("rows", "aux"), P(), P())
    return jax.shard_map(
        local,
        mesh=mesh,
        in_specs=placed,
        out_specs=(P("rows", "aux"), P(("rows", "aux"))),
        check_vma=False,
    )
```

time: 1390 us -> 69 us (0.05)
  waiting for transfers between devices: 1270 us -> 0 us
  blocking collectives: 108 us -> 0 us
  Pallas kernels: 0 us -> 65.7 us
  between operations: 14.7 us -> 0.65 us
    psum x1 -> x0, waiting for transfers between devices: 1270 us -> none  [local(): projected = lax.psum(partial_projection, 'rows')]
    unnamed x1 -> x0, blocking collectives: 73.6 us -> none
    pallas_call x0 -> x1, Pallas kernels: none -> 65.7 us  [local(): pl.pallas_call(kernel, out_shape=(jax.ShapeDtypeStruct((512, 256), F32),...]
    all_gather x1 -> x0, blocking collectives: 34.1 us -> none  [local(): chol_basis = lax.all_gather(cholesky_factors, 'aux', axis=1, tiled=True)]
  transfers between devices with their start and end apart: 1 -> 0, of which waited for: 1 -> 0; matrix products, arithmetic and copies ran while one was open for 0% -> 0% of each run, Pallas kernels for 0% -> 0%
where the time goes in v1:
time: 69 us; the launch traced here: 68.8 us
  Pallas kernels  65.7 us (95%)
  local copies, waits for them, and re-layouts  2.38 us (3%)
    pallas_call x1, Pallas kernels, local(): pl.pallas_call(kernel, out_shape=(jax.ShapeDtypeStruct((512, 256), F32),...  65.7 us
    unnamed x4, local copies, waits for them, and re-layouts  2.38 us

profile of v1, /device:TPU:1, one launch (start us, length us, event | category | flops | bytes accessed | tf_op | source)
XLA Modules:
  0.0 68.8 jit_solution(11117709293517813990)
XLA Ops:
  0.6 65.7 %shard_map.59 = (f32[512,256]{1,0:T(8,128)}, f32[1,64]{1,0:T(1,128)}) custom-call(bf16[512,256]{1,0:T(8,128)(2,1)} %green_block.1, bf16[64,512]{1,0:T(8,128)(2,1)} %bitcast.3, f32[256,256]{1,0:T(8,128)} %green_one.1, f32[4,128]{1,0:T(4,128)} %bitcast.4), custom_call_target="tpu_custom_call" | custom-call | tf_op jit(solution)/shard_map/pallas_call | solution.py:251
  66.4 0.0 copy-start
  66.4 1.9 %copy.8 = f32[512,256]{1,0:T(8,128)} copy(f32[512,256]{1,0:T(8,128)} %get-tuple-element.8) | data formatting | bytes 1048576
  68.3 0.0 copy-done
  68.3 0.5 copy.9
Async XLA Ops:
  66.4 1.9 %copy-start = (f32[1,64]{1,0:T(1,128)S(1)}, f32[1,64]{1,0:T(1,128)}, u32[]{:S(2)}) copy-start(f32[1,64]{1,0:T(1,128)} %get-tuple-element.5) | copy-start | bytes 772

commit v2 on v1

v2 whole, which is shorter than its diff:
```python
import jax
import jax.numpy as jnp
from jax import lax
from jax.experimental import pallas as pl
from jax.experimental.pallas import tpu as pltpu
from jax.sharding import PartitionSpec as P

NX, NY, NZ, NH = 4, 8, 4, 4
CHUNKS = 4
F32, BF16 = jnp.float32, jnp.bfloat16
HIGHEST = lax.Precision.HIGHEST
MESH = pl.DeviceIdType.MESH
NT = (((1,), (1,)), ((), ()))
NN = (((1,), (0,)), ((), ()))


def dot(a, b, dims=NN, precision=None):
    return lax.dot_general(a, b, dims, precision=precision, preferred_element_type=F32)


def iota(shape, axis):
    return lax.broadcasted_iota(jnp.int32, shape, axis)


def gather_kernel(
    green_block_hbm, own_chol, green_one_hbm, screening_hbm, chol_p, dressed, collision,
    green_block, green_one, screening, chol_t, part, part_in, ysum, y_in, z_all, vec, vx, vy, vz, uvec, uc,
    in_sem, own_send, own_recv, pc_send, pc_recv, z_send, z_recv, r_send, ready, uc_send, uc_recv, u_send, u_recv,
    x_send, x_recv, y_send, y_recv, l_send, l_recv, gy_send, gy_recv, gx_send, gx_recv,
    vx_send, vx_recv, vy_send, vy_recv, vz_send, vz_recv,
):
    row, aux = lax.axis_index("rows"), lax.axis_index("aux")
    mx, my, mz = row // (NY * NZ), (row // NZ) % NY, row % NZ
    mh, core = aux // 2, aux % 2

    def at_x(j):
        return {"rows": (((mx + j) % NX) * NY + my) * NZ + mz, "aux": aux}

    def at_y(j):
        return {"rows": (mx * NY + (my + j) % NY) * NZ + mz, "aux": aux}

    def at_z(j):
        return {"rows": (mx * NY + my) * NZ + (mz + j) % NZ, "aux": aux}

    def at(h):
        return {"rows": row, "aux": h * 2 + core}

    mate = {"rows": row, "aux": mh * 2 + 1 - core}
    sent = []

    def copy(src, dst, send, recv, to):
        return pltpu.make_async_remote_copy(
            src_ref=src, dst_ref=dst, send_sem=send, recv_sem=recv, device_id=to, device_id_type=MESH
        )

    def send(*what, when=None):
        made = copy(*what)
        sent.append((made, when))
        if when is None:
            made.start()
        else:
            pl.when(when)(made.start)

    odd, upper_half = mh % 2, mh // 2
    even, second, last = mh % 2 == 0, mh == 1, mh == NH - 1
    passes = jnp.logical_and(even, core == upper_half)

    barrier = pltpu.get_barrier_semaphore()
    peers = [at_y(j) for j in (4, 3, 5, 2, 6, 1, 7)] + [at_z(j) for j in range(1, NZ)]
    peers += [at_x(j) for j in (2, 1, 3)] + [mate]

    @pl.when(mh < NH - 1)
    def _():
        for step in (1, 3):
            pl.semaphore_signal(barrier, inc=1, device_id=at((mh + step) % NH), device_id_type=MESH)

    for peer in peers:
        pl.semaphore_signal(barrier, inc=1, device_id=peer, device_id_type=MESH)
    loads = [
        pltpu.make_async_copy(own_chol, chol_t.at[0, core], in_sem.at[0]),
        pltpu.make_async_copy(green_one_hbm, green_one, in_sem.at[1]),
        pltpu.make_async_copy(screening_hbm, screening, in_sem.at[2]),
        pltpu.make_async_copy(green_block_hbm, green_block, in_sem.at[3]),
    ]
    for load in loads:
        load.start()
    for load in loads:
        load.wait()

    pick = (iota((8, 256), 1) == aux).astype(F32)
    column = dot(pick, green_one[...], NT, HIGHEST)
    trace_row = dot(column, green_one[...], NT, HIGHEST)

    def split(value):
        wide = jnp.broadcast_to(value, (16, value.shape[1]))
        high = wide.astype(BF16).astype(F32)
        mid = (wide - high).astype(BF16).astype(F32)
        rest = wide - high - mid
        at_row = iota(wide.shape, 0)
        picked = jnp.where(at_row == 0, high, jnp.where(at_row == 1, mid, jnp.where(at_row == 2, rest, 0.0)))
        return picked.astype(BF16)

    def exact(value, right, dims):
        return jnp.sum(dot(split(value), right, dims), axis=0, keepdims=True)

    homes = (mh, 1 - odd, 2 - 2 * upper_half * (1 - odd), 3 - 2 * upper_half * odd)
    sub, lane = iota((8, 128), 0), iota((8, 128), 1)
    top = sub < 4

    own_first = 4 * (mx * NY + my)
    weights = [screening[pl.ds(home, 1), :] for home in homes]
    scales = [
        jnp.sum(jnp.where(lane == own_first + sub % 4, jnp.broadcast_to(w, (8, 128)), 0.0), axis=1, keepdims=True)
        for w in weights
    ]

    traced_rows = exact(trace_row[0:1, :], green_block[...], NT)
    tile = jnp.zeros((8, 128), F32)
    for r in range(4):
        tile = jnp.where(sub == r, jnp.broadcast_to(traced_rows[:, 128 * r : 128 * r + 128], (8, 128)), tile)
    uc[0] = tile

    pl.semaphore_wait(barrier, len(peers) + 1 + odd)

    @pl.when(last)
    def _():
        for h in (0, 2):
            pl.semaphore_signal(ready, inc=1, device_id=at(h), device_id_type=MESH)

    size = 64 // CHUNKS

    def block(t, i):
        return chol_t.at[t, core, pl.ds(i * size, size)]

    first_to, first_slot = 1 - odd, (1 - odd) * (1 + upper_half) + odd * mh
    for i in range(CHUNKS):
        send(block(0, i), block(first_slot, i), z_send.at[0, i], z_recv.at[first_slot, i], at(first_to))
        send(block(0, i), block(mh, i), z_send.at[1, i], z_recv.at[mh, i], at(2), when=odd == 1)
    send(chol_t.at[0, core], chol_t.at[0, core], own_send, own_recv, mate)
    send(uc.at[0], uc.at[1], uc_send, uc_recv, mate)

    def arrive(t, to=None, slot=None, when=None, u_when=None):
        for i in range(CHUNKS):
            here = block(t, i)
            copy(here, here, r_send.at[t, i], z_recv.at[t, i], mate).wait_recv()
            send(here, here, pc_send.at[t, i], pc_recv.at[t, i], mate)
            send(here, block(slot, i), r_send.at[t, i], z_recv.at[slot, i], at(to), when=when)
        copy(uvec.at[t], uvec.at[t], u_send.at[t], u_recv.at[t], mate).wait_recv()
        send(uvec.at[t], uvec.at[slot], u_send.at[t], u_recv.at[slot], at(to), when=u_when)

    def from_mate(t):
        for i in range(CHUNKS):
            there = chol_t.at[t, 1 - core, pl.ds(i * size, size)]
            copy(there, there, pc_send.at[t, i], pc_recv.at[t, i], mate).wait_recv()

    def project(t):
        product = dot(chol_t[t].reshape(128, 512), green_block[...])
        for j in range(16):
            left, right = product[8 * j : 8 * j + 8, :128], product[8 * j : 8 * j + 8, 128:]
            for e in range(2):
                g = 2 * j + e
                if e == 0:
                    tile = jnp.where(top, left, pltpu.roll(right, 4, 0))
                else:
                    tile = jnp.where(top, pltpu.roll(left, 4, 0), right)
                part[t, g // NY, g % NY] = tile
        for j in (2, 1, 3):
            send(part.at[t, (mx + j) % NX], part_in.at[t, j], x_send.at[t, j], x_recv.at[t, j], at_x(j))

    def sum_x(t):
        total = part[t, mx]
        for j in range(1, NX):
            copy(part_in.at[t, j], part_in.at[t, j], x_send.at[t, j], x_recv.at[t, j], mate).wait_recv()
            total = total + part_in[t, j]
        ysum[t] = total
        for j in (4, 3, 5, 2, 6, 1, 7):
            send(ysum.at[t, (my + j) % NY], y_in.at[t, j], y_send.at[t, j], y_recv.at[t, j], at_y(j))

    def sum_y(t):
        total = ysum[t, my]
        for j in range(1, NY):
            copy(y_in.at[t, j], y_in.at[t, j], y_send.at[t, j], y_recv.at[t, j], mate).wait_recv()
            total = total + y_in[t, j]
        z_all[mz, t] = total
        for j in range(1, NZ):
            send(z_all.at[mz, t], z_all.at[mz, t], l_send.at[t, j], l_recv.at[t, j], at_z(j))

    def spread(value, store, sems, count, to):
        store[0] = value
        for j in range(1, count):
            send(store.at[0], store.at[j], sems[0].at[j], sems[1].at[j], to(j))

    def collect(store, sems, count):
        total = store[0]
        for j in range(1, count):
            copy(store.at[j], store.at[j], sems[0].at[j], sems[1].at[j], mate).wait_recv()
            total = total + store[j]
        return total

    there = chol_t.at[0, 1 - core]
    copy(there, there, own_send, own_recv, mate).wait_recv()
    project(0)
    copy(uc.at[1], uc.at[1], uc_send, uc_recv, mate).wait_recv()
    uvec[0] = uc[0] + uc[1]
    send(uvec.at[0], uvec.at[first_slot], u_send.at[4], u_recv.at[first_slot], at(first_to))
    send(uvec.at[0], uvec.at[mh], u_send.at[5], u_recv.at[mh], at(2), when=odd == 1)

    arrive(1, 2, 2, second, second)
    from_mate(1)
    project(1)
    arrive(2, 0, 2, second, second)
    from_mate(2)
    project(2)

    @pl.when(even)
    def _():
        pl.semaphore_wait(ready, 1)

    late_slot = 1 + upper_half
    for i in range(CHUNKS):
        send(block(0, i), block(late_slot, i), z_send.at[2, i], z_recv.at[late_slot, i], at(3), when=even)
        send(block(1, i), block(3, i), z_send.at[3, i], z_recv.at[3, i], at(3), when=passes)
    send(uvec.at[0], uvec.at[late_slot], u_send.at[6], u_recv.at[late_slot], at(3), when=even)
    send(uvec.at[1], uvec.at[3], u_send.at[7], u_recv.at[3], at(3), when=mh == 0)
    sum_x(0)
    sum_x(1)
    sum_y(0)
    arrive(3, 1, 3, passes, mh == 0)
    from_mate(3)
    project(3)

    all_rows = (uvec[0] + uvec[1]) + (uvec[2] + uvec[3])
    all_row = jnp.concatenate([all_rows[r : r + 1, :] for r in range(4)], axis=1)
    tile = jnp.zeros((8, 128), F32)
    for t in range(4):
        tile = jnp.where(sub == t, jnp.broadcast_to(exact(all_row, chol_t[t].reshape(128, 512), NT), (8, 128)), tile)
    sems_vx, sems_vy, sems_vz = (vx_send, vx_recv), (vy_send, vy_recv), (vz_send, vz_recv)
    spread(tile, vx, sems_vx, NX, at_x)
    sum_x(2)
    sum_x(3)
    spread(collect(vx, sems_vx, NX), vy, sems_vy, NY, at_y)

    for b in range(4):
        new = iota((128, 512), 0) + 128 * b
        old = ((new >> 2) & 3) * 128 + (new >> 7) * 32 + ((new >> 4) & 7) * 4 + (new & 3)
        move = jnp.where(iota((128, 512), 1) == old, 1.0, 0.0).astype(BF16)
        moved = dot(move, chol_t[...].reshape(512, 512))
        chol_p[:, 128 * b : 128 * b + 128] = moved.T.astype(BF16)

    sum_y(1)
    sum_y(2)
    sum_y(3)
    spread(collect(vy, sems_vy, NY), vz, sems_vz, NZ, at_z)

    for t in range(4):
        for j in range(1, NZ):
            there = z_all.at[(mz + NZ - j) % NZ, t]
            copy(there, there, l_send.at[t, j], l_recv.at[t, j], mate).wait_recv()
    total = (z_all[0] + z_all[1]) + (z_all[2] + z_all[3])
    flat = total.reshape(32, 128)
    upper = dot(flat, green_one[:128, :], NN, HIGHEST)
    lower = dot(flat, green_one[128:, :], NN, HIGHEST)
    done = []
    for t in range(4):
        both = upper[8 * t : 8 * t + 8] + pltpu.roll(lower[8 * t : 8 * t + 8], 4, 0)
        done.append(both * scales[t])
    top2 = iota((8, 256), 0) < 4
    first = jnp.where(top2, done[0], pltpu.roll(done[1], 4, 0))
    second = jnp.where(top2, done[2], pltpu.roll(done[3], 4, 0))
    dressed[mx, my] = jnp.concatenate([first, second], axis=0).astype(BF16)

    def along_x(j):
        here = dressed.at[mx, (my + NY - j) % NY]
        for i in (2, 1, 3):
            send(here, here, gx_send.at[j, i], gx_recv.at[j, i], at_x(i))

    order = (1, 7, 2, 6, 3, 5, 4)
    here = dressed.at[mx, my]
    for j in order[::-1]:
        send(here, here, gy_send.at[j], gy_recv.at[j], at_y(j))
    along_x(0)
    vec[...] = collect(vz, sems_vz, NZ)
    traced = jnp.zeros((1, 512), F32)
    for t in range(4):
        traced = traced + exact(vec[t : t + 1, :] * weights[t], chol_t[t].reshape(128, 512), NN)
    for a in range(2 * NH):
        @pl.when(aux == a)
        def _():
            collision[...] = traced[:, 64 * a : 64 * a + 64]

    for j in order:
        there = dressed.at[mx, (my + NY - j) % NY]
        copy(there, there, gy_send.at[j], gy_recv.at[j], mate).wait_recv()
        along_x(j)

    for i in range(1, NX):
        for j in range(NY):
            there = dressed.at[(mx + NX - i) % NX, (my + NY - j) % NY]
            copy(there, there, gx_send.at[j, i], gx_recv.at[j, i], mate).wait_recv()

    for made, when in sent:
        if when is None:
            made.wait_send()
        else:
            pl.when(when)(made.wait_send)


SEMS = (
    (4,), (), (), (4, CHUNKS), (4, CHUNKS), (4, CHUNKS), (4, CHUNKS), (4, CHUNKS), None, (), (), (8,), (4,),
    (4, NX), (4, NX), (4, NY), (4, NY), (4, NZ), (4, NZ), (NY,), (NY,), (NY, NX), (NY, NX),
    (NX,), (NX,), (NY,), (NY,), (NZ,), (NZ,),
)


def local(pair_green_block, cholesky_factors, green_one, screening):
    vmem, dma = pltpu.VMEM, pltpu.SemaphoreType.DMA
    tile = (8, 128)
    chol_p, dressed, collision = pl.pallas_call(
        gather_kernel,
        out_shape=(
            pltpu.VMEM((512, 512), BF16),
            pltpu.VMEM((NX, NY, 16, 256), BF16),
            pltpu.VMEM((1, 64), F32),
        ),
        in_specs=[pl.BlockSpec(memory_space=pl.ANY)] * 4,
        out_specs=(pl.BlockSpec(memory_space=vmem),) * 3,
        scratch_shapes=[
            vmem((512, 256), BF16), vmem((256, 256), F32), vmem((4, 128), F32),
            vmem((4, 2, 64, 512), BF16),
            vmem((4, NX, NY) + tile, F32),
            vmem((4, NX, NY) + tile, F32),
            vmem((4, NY) + tile, F32),
            vmem((4, NY) + tile, F32),
            vmem((NZ, 4) + tile, F32),
            vmem(tile, F32),
            vmem((NX,) + tile, F32), vmem((NY,) + tile, F32), vmem((NZ,) + tile, F32), vmem((4,) + tile, F32), vmem((2,) + tile, F32),
        ] + [pltpu.SemaphoreType.REGULAR if shape is None else dma(shape) for shape in SEMS],
        compiler_params=pltpu.CompilerParams(collective_id=0, has_side_effects=True),
    )(pair_green_block, cholesky_factors.T, green_one, screening.reshape(4, 128))
    slope = jnp.dot(chol_p, dressed.reshape(512, 256), preferred_element_type=F32)
    return slope, collision.reshape(64)


def solution(mesh):
    placed = (P("rows", "aux"), P("rows", "aux"), P(), P())
    return jax.shard_map(
        local,
        mesh=mesh,
        in_specs=placed,
        out_specs=(P("rows", "aux"), P(("rows", "aux"))),
        check_vma=False,
    )
```

time: 69 us -> 67.5 us (0.978)
  the two profiles are of different devices: /device:TPU:1 before, /device:TPU:256 now
where the time goes in v2:
time: 67.5 us; the launch traced here: 67.4 us
  Pallas kernels  65.1 us (96%)
  matrix products  1.09 us (2%)
    pallas_call x1, Pallas kernels, local(): pl.pallas_call(gather_kernel, out_shape=(pltpu.VMEM((512, 512), BF16), pl...  65.1 us

profile of v2, /device:TPU:256, one launch (start us, length us, event | category | flops | bytes accessed | tf_op | source)
XLA Modules:
  0.0 67.4 jit_solution(4896149595434041954)
XLA Ops:
  0.6 65.1 %shard_map.59 = (bf16[512,512]{1,0:T(8,128)(2,1)S(1)}, bf16[4,8,16,256]{3,2,1,0:T(8,128)(2,1)S(1)}, f32[1,64]{1,0:T(1,128)S(1)}) custom-call(bf16[512,256]{1,0:T(8,128)(2,1)} %green_block_hbm.1, bf16[64,512]{1,0:T(8,128)(2,1)} %bitcast.8, f32[256,256]{1,0:T(8,128)} %green_one_hbm.1, f32[4,128]{1,0:T(4,128)} %bitcast.9), custom_call_target="tpu_custom_call" | custom-call | tf_op jit(solution)/shard_map/pallas_call | solution.py:318
  65.8 1.1 %fusion = f32[512,256]{1,0:T(8,128)} fusion(bf16[512,512]{1,0:T(8,128)(2,1)S(1)} %get-tuple-element.5, bf16[512,256]{1,0:T(8,128)(2,1)S(1)} %bitcast.7), kind=kOutput, calls=%fused_computation | convolution fusion | flops 134217728 | bytes 1310720 | tf_op jit(solution)/shard_map/dot_general | solution.py:340
  66.9 0.5 copy.7

commit v3 on v2

--- a/solution.py
+++ b/solution.py
@@ -6,7 +6,7 @@
 from jax.sharding import PartitionSpec as P
 
 NX, NY, NZ, NH = 4, 8, 4, 4
-CHUNKS = 4
+CHUNKS = 2
 F32, BF16 = jnp.float32, jnp.bfloat16
 HIGHEST = lax.Precision.HIGHEST
 MESH = pl.DeviceIdType.MESH
@@ -25,7 +25,7 @@
 def gather_kernel(
     green_block_hbm, own_chol, green_one_hbm, screening_hbm, chol_p, dressed, collision,
     green_block, green_one, screening, chol_t, part, part_in, ysum, y_in, z_all, vec, vx, vy, vz, uvec, uc,
-    in_sem, own_send, own_recv, pc_send, pc_recv, z_send, z_recv, r_send, ready, uc_send, uc_recv, u_send, u_recv,
+    in_sem, own_send, own_recv, pc_send, pc_recv, z_send, z_recv, f_send, uc_send, uc_recv, u_send, u_recv,
     x_send, x_recv, y_send, y_recv, l_send, l_recv, gy_send, gy_recv, gx_send, gx_recv,
     vx_send, vx_recv, vy_send, vy_recv, vz_send, vz_recv,
 ):
@@ -42,8 +42,8 @@
     def at_z(j):
         return {"rows": (mx * NY + my) * NZ + (mz + j) % NZ, "aux": aux}
 
-    def at(h):
-        return {"rows": row, "aux": h * 2 + core}
+    def at_h(j):
+        return {"rows": row, "aux": ((mh + j) % NH) * 2 + core}
 
     mate = {"rows": row, "aux": mh * 2 + 1 - core}
     sent = []
@@ -53,27 +53,15 @@
             src_ref=src, dst_ref=dst, send_sem=send, recv_sem=recv, device_id=to, device_id_type=MESH
         )
 
-    def send(*what, when=None):
+    def send(*what):
         made = copy(*what)
-        sent.append((made, when))
-        if when is None:
-            made.start()
-        else:
-            pl.when(when)(made.start)
-
-    odd, upper_half = mh % 2, mh // 2
-    even, second, last = mh % 2 == 0, mh == 1, mh == NH - 1
-    passes = jnp.logical_and(even, core == upper_half)
+        made.start()
+        sent.append(made)
+        return made
 
     barrier = pltpu.get_barrier_semaphore()
-    peers = [at_y(j) for j in (4, 3, 5, 2, 6, 1, 7)] + [at_z(j) for j in range(1, NZ)]
-    peers += [at_x(j) for j in (2, 1, 3)] + [mate]
-
-    @pl.when(mh < NH - 1)
-    def _():
-        for step in (1, 3):
-            pl.semaphore_signal(barrier, inc=1, device_id=at((mh + step) % NH), device_id_type=MESH)
-
+    peers = [at_h(1), at_h(NH - 1)] + [at_y(j) for j in (4, 3, 5, 2, 6, 1, 7)]
+    peers += [at_z(j) for j in range(1, NZ)] + [at_x(j) for j in (2, 1, 3)] + [mate]
     for peer in peers:
         pl.semaphore_signal(barrier, inc=1, device_id=peer, device_id_type=MESH)
     loads = [
@@ -84,6 +72,17 @@
     ]
     for load in loads:
         load.start()
+    pl.semaphore_wait(barrier, len(peers))
+
+    size = 64 // CHUNKS
+    onward, back = at_h(1 + 2 * core), at_h(3 - 2 * core)
+    for i in range(CHUNKS):
+        span = pl.ds(i * size, size)
+        mine = own_chol.at[span]
+        send(mine, chol_t.at[1, core, span], z_send.at[0, i], z_recv.at[1, i], onward)
+        send(mine, chol_t.at[2, core, span], z_send.at[1, i], z_recv.at[2, i], back)
+    send(own_chol, chol_t.at[0, core], own_send, own_recv, mate)
+
     for load in loads:
         load.wait()
 
@@ -103,50 +102,34 @@
     def exact(value, right, dims):
         return jnp.sum(dot(split(value), right, dims), axis=0, keepdims=True)
 
-    homes = (mh, 1 - odd, 2 - 2 * upper_half * (1 - odd), 3 - 2 * upper_half * odd)
+    before, after, across = (mh + NH - 1) % NH, (mh + 1) % NH, (mh + 2) % NH
+    homes = ((mh, mh), (before, after), (after, before), (across, across))
     sub, lane = iota((8, 128), 0), iota((8, 128), 1)
-    top = sub < 4
+    top, low = sub < 4, lane < 64
+
+    def by_piece(t, read):
+        first = jnp.broadcast_to(read(homes[t][0]), (8, 128))
+        second = jnp.broadcast_to(read(homes[t][1]), (8, 128))
+        return jnp.where(low, first, second)
 
     own_first = 4 * (mx * NY + my)
-    weights = [screening[pl.ds(home, 1), :] for home in homes]
-    scales = [
-        jnp.sum(jnp.where(lane == own_first + sub % 4, jnp.broadcast_to(w, (8, 128)), 0.0), axis=1, keepdims=True)
-        for w in weights
-    ]
+    weights = [by_piece(t, lambda h: screening[pl.ds(h, 1), :]) for t in range(4)]
+    scales = [jnp.sum(jnp.where(lane == own_first + sub % 4, w, 0.0), axis=1, keepdims=True) for w in weights]
 
     traced_rows = exact(trace_row[0:1, :], green_block[...], NT)
     tile = jnp.zeros((8, 128), F32)
     for r in range(4):
         tile = jnp.where(sub == r, jnp.broadcast_to(traced_rows[:, 128 * r : 128 * r + 128], (8, 128)), tile)
     uc[0] = tile
-
-    pl.semaphore_wait(barrier, len(peers) + 1 + odd)
-
-    @pl.when(last)
-    def _():
-        for h in (0, 2):
-            pl.semaphore_signal(ready, inc=1, device_id=at(h), device_id_type=MESH)
-
-    size = 64 // CHUNKS
-
-    def block(t, i):
-        return chol_t.at[t, core, pl.ds(i * size, size)]
-
-    first_to, first_slot = 1 - odd, (1 - odd) * (1 + upper_half) + odd * mh
-    for i in range(CHUNKS):
-        send(block(0, i), block(first_slot, i), z_send.at[0, i], z_recv.at[first_slot, i], at(first_to))
-        send(block(0, i), block(mh, i), z_send.at[1, i], z_recv.at[mh, i], at(2), when=odd == 1)
-    send(chol_t.at[0, core], chol_t.at[0, core], own_send, own_recv, mate)
     send(uc.at[0], uc.at[1], uc_send, uc_recv, mate)
 
-    def arrive(t, to=None, slot=None, when=None, u_when=None):
-        for i in range(CHUNKS):
-            here = block(t, i)
-            copy(here, here, r_send.at[t, i], z_recv.at[t, i], mate).wait_recv()
-            send(here, here, pc_send.at[t, i], pc_recv.at[t, i], mate)
-            send(here, block(slot, i), r_send.at[t, i], z_recv.at[slot, i], at(to), when=when)
-        copy(uvec.at[t], uvec.at[t], u_send.at[t], u_recv.at[t], mate).wait_recv()
-        send(uvec.at[t], uvec.at[slot], u_send.at[t], u_recv.at[slot], at(to), when=u_when)
+    def await_z(t, i):
+        here = chol_t.at[t, core, pl.ds(i * size, size)]
+        copy(here, here, f_send.at[i], z_recv.at[t, i], mate).wait_recv()
+        return here
+
+    def to_mate(t, i, here):
+        send(here, here, pc_send.at[t, i], pc_recv.at[t, i], mate)
 
     def from_mate(t):
         for i in range(CHUNKS):
@@ -154,9 +137,9 @@
             copy(there, there, pc_send.at[t, i], pc_recv.at[t, i], mate).wait_recv()
 
     def project(t):
-        product = dot(chol_t[t].reshape(128, 512), green_block[...])
+        block = dot(chol_t[t].reshape(128, 512), green_block[...])
         for j in range(16):
-            left, right = product[8 * j : 8 * j + 8, :128], product[8 * j : 8 * j + 8, 128:]
+            left, right = block[8 * j : 8 * j + 8, :128], block[8 * j : 8 * j + 8, 128:]
             for e in range(2):
                 g = 2 * j + e
                 if e == 0:
@@ -197,35 +180,34 @@
             total = total + store[j]
         return total
 
+    def await_u(t):
+        copy(uvec.at[t], uvec.at[t], u_send.at[0], u_recv.at[t], mate).wait_recv()
+
     there = chol_t.at[0, 1 - core]
     copy(there, there, own_send, own_recv, mate).wait_recv()
     project(0)
     copy(uc.at[1], uc.at[1], uc_send, uc_recv, mate).wait_recv()
     uvec[0] = uc[0] + uc[1]
-    send(uvec.at[0], uvec.at[first_slot], u_send.at[4], u_recv.at[first_slot], at(first_to))
-    send(uvec.at[0], uvec.at[mh], u_send.at[5], u_recv.at[mh], at(2), when=odd == 1)
-
-    arrive(1, 2, 2, second, second)
+    send(uvec.at[0], uvec.at[1], u_send.at[0], u_recv.at[1], at_h(1))
+    send(uvec.at[0], uvec.at[2], u_send.at[1], u_recv.at[2], at_h(3))
+
+    for i in range(CHUNKS):
+        here = await_z(1, i)
+        send(here, chol_t.at[3, core, pl.ds(i * size, size)], f_send.at[i], z_recv.at[3, i], onward)
+        to_mate(1, i, here)
+    await_u(1)
+    send(uvec.at[1], uvec.at[3], u_send.at[2], u_recv.at[3], at_h(1))
+    for i in range(CHUNKS):
+        to_mate(2, i, await_z(2, i))
+    await_u(2)
     from_mate(1)
     project(1)
-    arrive(2, 0, 2, second, second)
     from_mate(2)
     project(2)
-
-    @pl.when(even)
-    def _():
-        pl.semaphore_wait(ready, 1)
-
-    late_slot = 1 + upper_half
+    sum_x(0)
     for i in range(CHUNKS):
-        send(block(0, i), block(late_slot, i), z_send.at[2, i], z_recv.at[late_slot, i], at(3), when=even)
-        send(block(1, i), block(3, i), z_send.at[3, i], z_recv.at[3, i], at(3), when=passes)
-    send(uvec.at[0], uvec.at[late_slot], u_send.at[6], u_recv.at[late_slot], at(3), when=even)
-    send(uvec.at[1], uvec.at[3], u_send.at[7], u_recv.at[3], at(3), when=mh == 0)
-    sum_x(0)
-    sum_x(1)
-    sum_y(0)
-    arrive(3, 1, 3, passes, mh == 0)
+        to_mate(3, i, await_z(3, i))
+    await_u(3)
     from_mate(3)
     project(3)
 
@@ -236,8 +218,10 @@
         tile = jnp.where(sub == t, jnp.broadcast_to(exact(all_row, chol_t[t].reshape(128, 512), NT), (8, 128)), tile)
     sems_vx, sems_vy, sems_vz = (vx_send, vx_recv), (vy_send, vy_recv), (vz_send, vz_recv)
     spread(tile, vx, sems_vx, NX, at_x)
+    sum_x(1)
     sum_x(2)
     sum_x(3)
+    sum_y(0)
     spread(collect(vx, sems_vx, NX), vy, sems_vy, NY, at_y)
 
     for b in range(4):
@@ -280,33 +264,30 @@
         send(here, here, gy_send.at[j], gy_recv.at[j], at_y(j))
     along_x(0)
     vec[...] = collect(vz, sems_vz, NZ)
+    for j in order:
+        there = dressed.at[mx, (my + NY - j) % NY]
+        copy(there, there, gy_send.at[j], gy_recv.at[j], mate).wait_recv()
+        along_x(j)
+
     traced = jnp.zeros((1, 512), F32)
     for t in range(4):
-        traced = traced + exact(vec[t : t + 1, :] * weights[t], chol_t[t].reshape(128, 512), NN)
+        traced = traced + exact(vec[t : t + 1, :] * weights[t][0:1, :], chol_t[t].reshape(128, 512), NN)
     for a in range(2 * NH):
         @pl.when(aux == a)
         def _():
             collision[...] = traced[:, 64 * a : 64 * a + 64]
 
-    for j in order:
-        there = dressed.at[mx, (my + NY - j) % NY]
-        copy(there, there, gy_send.at[j], gy_recv.at[j], mate).wait_recv()
-        along_x(j)
-
     for i in range(1, NX):
         for j in range(NY):
             there = dressed.at[(mx + NX - i) % NX, (my + NY - j) % NY]
             copy(there, there, gx_send.at[j, i], gx_recv.at[j, i], mate).wait_recv()
 
-    for made, when in sent:
-        if when is None:
-            made.wait_send()
-        else:
-            pl.when(when)(made.wait_send)
+    for made in sent:
+        made.wait_send()
 
 
 SEMS = (
-    (4,), (), (), (4, CHUNKS), (4, CHUNKS), (4, CHUNKS), (4, CHUNKS), (4, CHUNKS), None, (), (), (8,), (4,),
+    (4,), (), (), (4, CHUNKS), (4, CHUNKS), (2, CHUNKS), (4, CHUNKS), (CHUNKS,), (), (), (3,), (4,),
     (4, NX), (4, NX), (4, NY), (4, NY), (4, NZ), (4, NZ), (NY,), (NY,), (NY, NX), (NY, NX),
     (NX,), (NX,), (NY,), (NY,), (NZ,), (NZ,),
 )
@@ -333,8 +314,9 @@
             vmem((4, NY) + tile, F32),
             vmem((NZ, 4) + tile, F32),
             vmem(tile, F32),
-            vmem((NX,) + tile, F32), vmem((NY,) + tile, F32), vmem((NZ,) + tile, F32), vmem((4,) + tile, F32), vmem((2,) + tile, F32),
-        ] + [pltpu.SemaphoreType.REGULAR if shape is None else dma(shape) for shape in SEMS],
+            vmem((NX,) + tile, F32), vmem((NY,) + tile, F32), vmem((NZ,) + tile, F32), vmem((4,) + tile, F32),
+            vmem((2,) + tile, F32),
+        ] + [dma(shape) for shape in SEMS],
         compiler_params=pltpu.CompilerParams(collective_id=0, has_side_effects=True),
     )(pair_green_block, cholesky_factors.T, green_one, screening.reshape(4, 128))
     slope = jnp.dot(chol_p, dressed.reshape(512, 256), preferred_element_type=F32)

time: 67.5 us -> 62.4 us (0.924)
  the two profiles are of different devices: /device:TPU:256 before, /device:TPU:8 now
where the time goes in v3:
time: 62.4 us; the launch traced here: 62.3 us
  Pallas kernels  60.1 us (96%)
  matrix products  1.09 us (2%)
  between operations  0.64 us (1%)
    pallas_call x1, Pallas kernels, local(): pl.pallas_call(gather_kernel, out_shape=(pltpu.VMEM((512, 512), BF16), pl...  60.1 us

profile of v3, /device:TPU:8, one launch (start us, length us, event | category | flops | bytes accessed | tf_op | source)
XLA Modules:
  0.0 62.3 jit_solution(4078053564386647326)
XLA Ops:
  0.6 60.1 %shard_map.59 = (bf16[512,512]{1,0:T(8,128)(2,1)S(1)}, bf16[4,8,16,256]{3,2,1,0:T(8,128)(2,1)S(1)}, f32[1,64]{1,0:T(1,128)S(1)}) custom-call(bf16[512,256]{1,0:T(8,128)(2,1)} %green_block_hbm.1, bf16[64,512]{1,0:T(8,128)(2,1)} %bitcast.8, f32[256,256]{1,0:T(8,128)} %green_one_hbm.1, f32[4,128]{1,0:T(4,128)} %bitcast.9), custom_call_target="tpu_custom_call" | custom-call | tf_op jit(solution)/shard_map/pallas_call | solution.py:299
  60.7 1.1 %fusion = f32[512,256]{1,0:T(8,128)} fusion(bf16[512,512]{1,0:T(8,128)(2,1)S(1)} %get-tuple-element.5, bf16[512,256]{1,0:T(8,128)(2,1)S(1)} %bitcast.7), kind=kOutput, calls=%fused_computation | convolution fusion | flops 134217728 | bytes 1310720 | tf_op jit(solution)/shard_map/dot_general | solution.py:322
  61.8 0.5 copy.7

commit v4 on v2

--- a/solution.py
+++ b/solution.py
@@ -6,7 +6,7 @@
 from jax.sharding import PartitionSpec as P
 
 NX, NY, NZ, NH = 4, 8, 4, 4
-CHUNKS = 4
+CHUNKS = 2
 F32, BF16 = jnp.float32, jnp.bfloat16
 HIGHEST = lax.Precision.HIGHEST
 MESH = pl.DeviceIdType.MESH
@@ -26,6 +26,7 @@
     green_block_hbm, own_chol, green_one_hbm, screening_hbm, chol_p, dressed, collision,
     green_block, green_one, screening, chol_t, part, part_in, ysum, y_in, z_all, vec, vx, vy, vz, uvec, uc,
     in_sem, own_send, own_recv, pc_send, pc_recv, z_send, z_recv, r_send, ready, uc_send, uc_recv, u_send, u_recv,
+    tok_x, tok_y, tok_z,
     x_send, x_recv, y_send, y_recv, l_send, l_recv, gy_send, gy_recv, gx_send, gx_recv,
     vx_send, vx_recv, vy_send, vy_recv, vz_send, vz_recv,
 ):
@@ -66,16 +67,22 @@
     passes = jnp.logical_and(even, core == upper_half)
 
     barrier = pltpu.get_barrier_semaphore()
-    peers = [at_y(j) for j in (4, 3, 5, 2, 6, 1, 7)] + [at_z(j) for j in range(1, NZ)]
-    peers += [at_x(j) for j in (2, 1, 3)] + [mate]
+    peers = [at_y(1), at_y(NY - 1), at_x(1), at_x(NX - 1), mate]
+    has_down, has_up = mz > 0, mz < NZ - 1
+    line = ((has_down, at_z(NZ - 1), 0), (has_up, at_z(1), 1))
+
+    def signal(sem, to):
+        pl.semaphore_signal(sem, inc=1, device_id=to, device_id_type=MESH)
 
     @pl.when(mh < NH - 1)
     def _():
         for step in (1, 3):
-            pl.semaphore_signal(barrier, inc=1, device_id=at((mh + step) % NH), device_id_type=MESH)
-
+            signal(barrier, at((mh + step) % NH))
+
+    for there, to, _ in line:
+        pl.when(there)(lambda to=to: signal(barrier, to))
     for peer in peers:
-        pl.semaphore_signal(barrier, inc=1, device_id=peer, device_id_type=MESH)
+        signal(barrier, peer)
     loads = [
         pltpu.make_async_copy(own_chol, chol_t.at[0, core], in_sem.at[0]),
         pltpu.make_async_copy(green_one_hbm, green_one, in_sem.at[1]),
@@ -84,6 +91,46 @@
     ]
     for load in loads:
         load.start()
+    inner = has_down.astype(jnp.int32) + has_up.astype(jnp.int32)
+    pl.semaphore_wait(barrier, len(peers) + 1 + odd + inner)
+
+    @pl.when(last)
+    def _():
+        for h in (0, 2):
+            signal(ready, at(h))
+
+    size = 64 // CHUNKS
+
+    def block(t, i):
+        return chol_t.at[t, core, pl.ds(i * size, size)]
+
+    first_to, first_slot = 1 - odd, (1 - odd) * (1 + upper_half) + odd * mh
+    for i in range(CHUNKS):
+        mine = own_chol.at[pl.ds(i * size, size)]
+        send(mine, block(first_slot, i), z_send.at[0, i], z_recv.at[first_slot, i], at(first_to))
+    for i in range(CHUNKS):
+        mine = own_chol.at[pl.ds(i * size, size)]
+        send(mine, block(mh, i), z_send.at[1, i], z_recv.at[mh, i], at(2), when=odd == 1)
+    send(own_chol, chol_t.at[0, core], own_send, own_recv, mate)
+
+    def announce(y=True, z=True):
+        if y:
+            signal(tok_y.at[0], at_y(1))
+            signal(tok_y.at[1], at_y(NY - 1))
+        if z:
+            for there, to, side in line:
+                pl.when(there)(lambda to=to, side=side: signal(tok_z.at[side], to))
+
+    def heard(y=True, z=True):
+        if y:
+            pl.semaphore_wait(tok_y.at[0], 1)
+            pl.semaphore_wait(tok_y.at[1], 1)
+        if z:
+            for there, _, side in line:
+                pl.when(there)(lambda side=side: pl.semaphore_wait(tok_z.at[1 - side], 1))
+
+    signal(tok_x, at_x(1))
+    announce()
     for load in loads:
         load.wait()
 
@@ -120,24 +167,10 @@
         tile = jnp.where(sub == r, jnp.broadcast_to(traced_rows[:, 128 * r : 128 * r + 128], (8, 128)), tile)
     uc[0] = tile
 
-    pl.semaphore_wait(barrier, len(peers) + 1 + odd)
-
-    @pl.when(last)
-    def _():
-        for h in (0, 2):
-            pl.semaphore_signal(ready, inc=1, device_id=at(h), device_id_type=MESH)
-
-    size = 64 // CHUNKS
-
-    def block(t, i):
-        return chol_t.at[t, core, pl.ds(i * size, size)]
-
-    first_to, first_slot = 1 - odd, (1 - odd) * (1 + upper_half) + odd * mh
-    for i in range(CHUNKS):
-        send(block(0, i), block(first_slot, i), z_send.at[0, i], z_recv.at[first_slot, i], at(first_to))
-        send(block(0, i), block(mh, i), z_send.at[1, i], z_recv.at[mh, i], at(2), when=odd == 1)
-    send(chol_t.at[0, core], chol_t.at[0, core], own_send, own_recv, mate)
     send(uc.at[0], uc.at[1], uc_send, uc_recv, mate)
+    heard()
+    announce()
+    pl.semaphore_wait(tok_x, 1)
 
     def arrive(t, to=None, slot=None, when=None, u_when=None):
         for i in range(CHUNKS):
@@ -205,12 +238,12 @@
     send(uvec.at[0], uvec.at[first_slot], u_send.at[4], u_recv.at[first_slot], at(first_to))
     send(uvec.at[0], uvec.at[mh], u_send.at[5], u_recv.at[mh], at(2), when=odd == 1)
 
+    heard()
+    announce(z=False)
+    heard(z=False)
     arrive(1, 2, 2, second, second)
     from_mate(1)
     project(1)
-    arrive(2, 0, 2, second, second)
-    from_mate(2)
-    project(2)
 
     @pl.when(even)
     def _():
@@ -222,12 +255,13 @@
         send(block(1, i), block(3, i), z_send.at[3, i], z_recv.at[3, i], at(3), when=passes)
     send(uvec.at[0], uvec.at[late_slot], u_send.at[6], u_recv.at[late_slot], at(3), when=even)
     send(uvec.at[1], uvec.at[3], u_send.at[7], u_recv.at[3], at(3), when=mh == 0)
-    sum_x(0)
-    sum_x(1)
-    sum_y(0)
+    arrive(2, 0, 2, second, second)
     arrive(3, 1, 3, passes, mh == 0)
+    from_mate(2)
+    project(2)
     from_mate(3)
     project(3)
+    sum_x(0)
 
     all_rows = (uvec[0] + uvec[1]) + (uvec[2] + uvec[3])
     all_row = jnp.concatenate([all_rows[r : r + 1, :] for r in range(4)], axis=1)
@@ -236,8 +270,10 @@
         tile = jnp.where(sub == t, jnp.broadcast_to(exact(all_row, chol_t[t].reshape(128, 512), NT), (8, 128)), tile)
     sems_vx, sems_vy, sems_vz = (vx_send, vx_recv), (vy_send, vy_recv), (vz_send, vz_recv)
     spread(tile, vx, sems_vx, NX, at_x)
+    sum_x(1)
     sum_x(2)
     sum_x(3)
+    sum_y(0)
     spread(collect(vx, sems_vx, NX), vy, sems_vy, NY, at_y)
 
     for b in range(4):
@@ -306,14 +342,22 @@
 
 
 SEMS = (
-    (4,), (), (), (4, CHUNKS), (4, CHUNKS), (4, CHUNKS), (4, CHUNKS), (4, CHUNKS), None, (), (), (8,), (4,),
+    (4,), (), (), (4, CHUNKS), (4, CHUNKS), (4, CHUNKS), (4, CHUNKS), (4, CHUNKS), None, (), (), (8,), (4,), None, 2, 2,
     (4, NX), (4, NX), (4, NY), (4, NY), (4, NZ), (4, NZ), (NY,), (NY,), (NY, NX), (NY, NX),
     (NX,), (NX,), (NY,), (NY,), (NZ,), (NZ,),
 )
 
 
+def semaphores(shape):
+    if shape is None:
+        return pltpu.SemaphoreType.REGULAR
+    if isinstance(shape, int):
+        return pltpu.SemaphoreType.REGULAR((shape,))
+    return pltpu.SemaphoreType.DMA(shape)
+
+
 def local(pair_green_block, cholesky_factors, green_one, screening):
-    vmem, dma = pltpu.VMEM, pltpu.SemaphoreType.DMA
+    vmem = pltpu.VMEM
     tile = (8, 128)
     chol_p, dressed, collision = pl.pallas_call(
         gather_kernel,
@@ -334,7 +378,7 @@
             vmem((NZ, 4) + tile, F32),
             vmem(tile, F32),
             vmem((NX,) + tile, F32), vmem((NY,) + tile, F32), vmem((NZ,) + tile, F32), vmem((4,) + tile, F32), vmem((2,) + tile, F32),
-        ] + [pltpu.SemaphoreType.REGULAR if shape is None else dma(shape) for shape in SEMS],
+        ] + [semaphores(shape) for shape in SEMS],
         compiler_params=pltpu.CompilerParams(collective_id=0, has_side_effects=True),
     )(pair_green_block, cholesky_factors.T, green_one, screening.reshape(4, 128))
     slope = jnp.dot(chol_p, dressed.reshape(512, 256), preferred_element_type=F32)

time: 67.5 us -> 62.1 us (0.920)
  Pallas kernels: 65.1 us -> 59.6 us
    pallas_call x1, Pallas kernels: 65.1 us -> 59.6 us  [local(): pl.pallas_call(gather_kernel, out_shape=(pltpu.VMEM((512, 512), BF16), pl...]
where the time goes in v4:
time: 62.1 us; the launch traced here: 61.9 us
  Pallas kernels  59.6 us (96%)
  matrix products  1.1 us (2%)
  between operations  0.64 us (1%)
    pallas_call x1, Pallas kernels, local(): pl.pallas_call(gather_kernel, out_shape=(pltpu.VMEM((512, 512), BF16), pl...  59.6 us

profile of v4, /device:TPU:256, one launch (start us, length us, event | category | flops | bytes accessed | tf_op | source)
XLA Modules:
  0.0 61.9 jit_solution(16870711319473850954)
XLA Ops:
  0.6 59.6 %shard_map.59 = (bf16[512,512]{1,0:T(8,128)(2,1)S(1)}, bf16[4,8,16,256]{3,2,1,0:T(8,128)(2,1)S(1)}, f32[1,64]{1,0:T(1,128)S(1)}) custom-call(bf16[512,256]{1,0:T(8,128)(2,1)} %green_block_hbm.1, bf16[64,512]{1,0:T(8,128)(2,1)} %bitcast.8, f32[256,256]{1,0:T(8,128)} %green_one_hbm.1, f32[4,128]{1,0:T(4,128)} %bitcast.9), custom_call_target="tpu_custom_call" | custom-call | tf_op jit(solution)/shard_map/pallas_call | solution.py:362
  60.3 1.1 %fusion = f32[512,256]{1,0:T(8,128)} fusion(bf16[512,512]{1,0:T(8,128)(2,1)S(1)} %get-tuple-element.5, bf16[512,256]{1,0:T(8,128)(2,1)S(1)} %bitcast.7), kind=kOutput, calls=%fused_computation | convolution fusion | flops 134217728 | bytes 1310720 | tf_op jit(solution)/shard_map/dot_general | solution.py:384
  61.4 0.5 copy.7
